TPU v7x, 32 devices: a whole 2x2x4 slice. The times are simulated.
32 devices in a mesh: gx: 2 (over x), gy: 4 (over z), gz: 4 (over y, core).
Axes of the slice: x: 2, y: 2, z: 4, core: 2. Of those that a mesh axis runs over, the one named last changes fastest.
Arguments:
- spectrum: bfloat16 [64, 128, 32, 256], P('gx', 'gy', 'gz'), may hold values from 0.049804688 to 2
- wind_east: float32 [64, 128, 32], P('gx', 'gy', 'gz'), may hold values from -0.45 to 0.45
- wind_north: float32 [64, 128, 32], P('gx', 'gy', 'gz'), may hold values from -0.45 to 0.45
- fall_rate: float32 [32, 256], P('gz'), may hold values from 0.006 to 12
- cloud_cells: int32 [2, 4, 4, 64, 16], P('gx', 'gy', 'gz'), may hold values from 0 to 8191, as said below
- block_target: int32 [2, 4, 4, 64], P(None, None, 'gz'), may hold values from 0 to 8, as said below
- pair_inputs: bfloat16 [256, 2048], replicated, may hold values from -0.375 to 0.375
- pair_outputs: bfloat16 [1024, 256], replicated, may hold values from -0.1875 to 0.1875
- loss_kernel: bfloat16 [256, 256], replicated, may hold values from 0 to 0.00390625
- fragments: bfloat16 [256, 256], replicated, may hold values from 0 to 0.0078125
Outputs:
- settled: bfloat16 [64, 128, 32, 256], P('gx', 'gy', 'gz')
Inputs may be any that keep to these rules, and one draw needn't show every extreme that they name: `cloud_cells`: entry [i, j, k, b, :] lists the local cell numbers (x * 32 + y) * 8 + z of block b of the device at mesh index (i, j, k); the 1024 entries of one device are distinct. `block_target`: entry [i, j, k, b] below 8 is the flat index i2 * (devices along gy) + j2 of the device (i2, j2, k) that works on block b of device (i, j, k); 8 marks a block without cloud. In each gz index the cloudy blocks number 8 * 32 in all, a device holds 1 to 64 of them, every device of the plane is named exactly 32 times, and by at most 8 blocks of any one device.
All inputs are finite; a program needn't handle non-finite values.
Results may differ from a plain program's by a relative error of at most 0.0032.
Values may be sent and summed in bfloat16 or wider, within the bound.
A program may use at most 128 MiB of HBM per device.

v0:
```python
import functools

import jax
import jax.numpy as jnp
from jax import lax
from jax.experimental import pallas as pl
from jax.experimental.pallas import tpu as pltpu
from jax.sharding import PartitionSpec as P

MESH = pl.DeviceIdType.MESH
F32 = jnp.float32
BF16 = jnp.bfloat16
I32 = jnp.int32
LANES = 128


def step_kernel(
    spec, winds_e, winds_n, fall_h, cells_h, target_h, pair_in_h, pair_out_h, loss_h, frag_h,
    adv, moist, arrived, edge_in,
    local, we, wn, west, east, south, north, fall, cells, cells_v, target, pair_in, pair_out, loss, frag,
    rows, q, pz, ids, parts_p, flux, edge_flux, extra,
    load_sem, in_sem, send_sem, recv_sem, down_sem, got_sem,
):
    nx, ny, packed, _ = spec.shape
    nz, bins = fall.shape
    halves = bins // LANES
    width, blocks = cells.shape
    total = width * blocks
    pairs = pair_out.shape[0]
    parts = load_sem.shape[0]
    per = nx // parts
    gx, gy, me = lax.axis_index("gx"), lax.axis_index("gy"), lax.axis_index("gz")
    sx, sy, count = lax.axis_size("gx"), lax.axis_size("gy"), lax.axis_size("gz")
    plane = sx * sy
    top = count - 1
    to_west = {"gx": lax.rem(gx + sx - 1, sx)}
    to_east = {"gx": lax.rem(gx + 1, sx)}
    to_south = {"gy": lax.rem(gy + sy - 1, sy)}
    to_north = {"gy": lax.rem(gy + 1, sy)}
    above = {"gz": lax.rem(me + 1, count)}
    below = {"gz": lax.rem(me + top, count)}

    barrier = pltpu.get_barrier_semaphore()
    for peer in (to_west, to_east, to_south, to_north, above, below):
        pl.semaphore_signal(barrier, inc=1, device_id=peer, device_id_type=MESH)

    def fetch(i, src, dst):
        return pltpu.make_async_copy(src, dst, in_sem.at[i])

    wind_loads = [fetch(0, winds_e, we), fetch(1, winds_n, wn)]
    loads = [
        pltpu.make_async_copy(spec.at[pl.ds(p * per, per)], local.at[pl.ds(1 + p * per, per)], load_sem.at[p])
        for p in range(parts)
    ]
    small = [fetch(2, fall_h, fall), fetch(3, cells_h, cells), fetch(4, cells_h, cells_v), fetch(5, target_h, target)]
    weights = [
        fetch(6, pair_in_h, pair_in), fetch(7, pair_out_h, pair_out), fetch(8, loss_h, loss), fetch(9, frag_h, frag)
    ]
    for load in wind_loads + loads + small + weights:
        load.start()
    pl.semaphore_wait(barrier, 6)

    sends = [
        pltpu.make_async_remote_copy(
            src_ref=src,
            dst_ref=dst,
            send_sem=send_sem.at[i],
            recv_sem=recv_sem.at[i],
            device_id=peer,
            device_id_type=MESH,
        )
        for i, (src, dst, peer) in enumerate(
            (
                (spec.at[:, ny - 1], south, to_north),
                (spec.at[:, 0], north, to_south),
                (spec.at[nx - 1], west, to_east),
                (spec.at[0], east, to_west),
            )
        )
    ]
    for send in sends:
        send.start()

    zero_row = jnp.zeros((ny, packed, LANES), BF16)
    local[0] = zero_row
    local[nx + 1] = zero_row

    def spread(column):
        wide = jnp.broadcast_to(column, (nz, LANES))
        return jnp.concatenate([wide] * halves, axis=0).astype(BF16)

    def one_row(x, carry):
        east_w, north_w = we[x], wn[x]
        zero = jnp.zeros((packed, LANES), BF16)
        behind = zero
        centre = local[x + 1, 0]
        for y in range(ny):
            ahead = local[x + 1, y + 1] if y + 1 < ny else zero
            a, b = spread(east_w[:, y : y + 1]), spread(north_w[:, y : y + 1])
            up_x = jnp.where(a > 0, local[x, y], local[x + 2, y])
            up_y = jnp.where(b > 0, behind, ahead)
            change = jnp.abs(a) * (up_x - centre) + jnp.abs(b) * (up_y - centre)
            value = centre.astype(F32) + change.astype(F32)
            at = pl.ds(pl.multiple_of((x * ny + y) * nz, nz), nz)
            for h in range(halves):
                adv[h, at, :] = value[h * nz : (h + 1) * nz]
            behind, centre = centre, ahead
        return carry

    for load in wind_loads:
        load.wait()
    done = 0
    for p in range(parts):
        loads[p].wait()
        upto = nx if p == parts - 1 else (p + 1) * per - 1
        lax.fori_loop(done, upto, one_row, 0)
        done = upto

    for load in small:
        load.wait()

    ratio = fall[...] / (1.0 + fall[...])
    share = jnp.ones((1, bins), F32)
    for z in range(nz):
        share = share * ratio[z : z + 1, :]
        parts_p[z : z + 1, :] = share
    parts_p[nz : 2 * nz, :] = ratio
    gain = share

    listed = cells_v[...]
    cloudy = target[gx, gy] < plane
    columns = jnp.where(cloudy, listed // nz, -1)
    per_tile = LANES // blocks
    for t in range(total // LANES):
        ids[t : t + 1, :] = jnp.concatenate(
            [columns[t * per_tile + i : t * per_tile + i + 1, :] for i in range(per_tile)], axis=1
        )
    heights = (listed % nz).astype(F32).T
    high = parts_p[0:nz, :].astype(BF16)
    low = (parts_p[0:nz, :] - high.astype(F32)).astype(BF16)
    table = jnp.concatenate([high, low, jnp.zeros((LANES - 2 * nz, bins), BF16)], axis=0)
    lane = lax.broadcasted_iota(I32, (blocks, LANES), 1)
    level_of = jnp.where(lane < 2 * nz, lane % nz, -1).astype(F32)
    for j in range(width):
        pick = jnp.where(jnp.broadcast_to(heights[:, j : j + 1], (blocks, LANES)) == level_of, 1.0, 0.0).astype(BF16)
        pz[j * blocks : (j + 1) * blocks, :] = jnp.dot(pick, table, preferred_element_type=F32)

    for load in weights:
        load.wait()

    def gather(k, carry):
        for j in range(width):
            cell = pl.ds(cells[j, k], 1)
            for h in range(halves):
                rows[h, pl.ds(j * blocks + k, 1), :] = adv[h, cell, :]
        return carry

    size = min(256, total)
    tile = min(256, pairs)

    def collide(i, carry):
        at = pl.ds(pl.multiple_of(i * size, size), size)
        full = jnp.concatenate([rows[h, at, :] for h in range(halves)], axis=1)
        row = full.astype(BF16)
        decline = jnp.dot(row, loss[...], preferred_element_type=F32)
        losses = row.astype(F32) * decline
        gained = jnp.dot(losses.astype(BF16), frag[...], preferred_element_type=F32)
        for n in range(0, pairs, tile):
            first = jnp.dot(row, pair_in[:, n : n + tile], preferred_element_type=F32)
            second = jnp.dot(row, pair_in[:, pairs + n : pairs + n + tile], preferred_element_type=F32)
            product = (first * second).astype(BF16)
            gained = gained + jnp.dot(product, pair_out[n : n + tile, :], preferred_element_type=F32)
        tendency = (gained - losses).astype(BF16).astype(F32)
        q[at, :] = (tendency * pz[at, :]).astype(BF16)
        after = full + tendency
        for h in range(halves):
            moist[h, at, :] = after[:, h * LANES : (h + 1) * LANES]
        return carry

    def collide_all():
        lax.fori_loop(0, blocks, gather, 0)
        lax.fori_loop(0, total // size, collide, 0)

    def collected(column):
        hot = [
            jnp.where(jnp.broadcast_to(ids[t : t + 1, :], column.shape) == column, 1.0, 0.0).astype(BF16)
            for t in range(total // LANES)
        ]
        return jnp.dot(jnp.concatenate(hot, axis=1), q[...], preferred_element_type=F32)

    def drained(base, stride, at_lanes, h):
        inflow = jnp.zeros((8, LANES), F32)
        for z in reversed(range(nz)):
            level = adv[h, pl.ds(base + z, 8, stride=stride), :]
            inflow = (level + inflow) * parts_p[nz + z : nz + z + 1, at_lanes]
        return inflow

    inner = down_sem.shape[0] - 1
    span = (nx - 2) // inner
    wide = span * ny

    def down(p):
        src = edge_flux if p == inner else flux.at[pl.ds(p * wide, wide)]
        dst = edge_in if p == inner else arrived.at[pl.ds((1 + p * span) * ny, wide)]
        return pltpu.make_async_remote_copy(
            src_ref=src,
            dst_ref=dst,
            send_sem=down_sem.at[p],
            recv_sem=got_sem.at[p],
            device_id={"gz": jnp.maximum(me - 1, 0)},
            device_id_type=MESH,
        )

    def relay(p):
        down(p).wait_recv()

        @pl.when(me > 0)
        def _():
            if p == inner:
                edge_flux[...] = (edge_flux[...].astype(F32) + edge_in[...].astype(F32) * gain).astype(BF16)
            else:
                at = pl.ds(p * wide, wide)
                got = arrived[pl.ds((1 + p * span) * ny, wide), :].astype(F32)
                flux[at, :] = (flux[at, :].astype(F32) + got * gain).astype(BF16)
            down(p).start()

    collide_all()

    for p in range(inner):
        column = lax.broadcasted_iota(I32, (wide, LANES), 0) + (1 + p * span) * ny
        extra[0:wide, :] = collected(column)

        def drain(g, carry):
            at = pl.ds(pl.multiple_of(g * 8, 8), 8)
            base = pl.multiple_of(((1 + p * span) * ny + g * 8) * nz, 8 * nz)
            for h in range(halves):
                lanes = slice(h * LANES, (h + 1) * LANES)
                extra[at, lanes] = extra[at, lanes] + drained(base, nz, lanes, h)
            return carry

        lax.fori_loop(0, wide // 8, drain, 0, unroll=4)
        flux[p * wide : (p + 1) * wide, :] = extra[0:wide, :].astype(BF16)

        @pl.when(me == top)
        def _():
            down(p).start()

        @pl.when(me == top - 1)
        def _():
            relay(p)

    for send in sends[:2]:
        send.wait_recv()

    def edges(x, carry):
        for y, halo, sign in ((0, south, 1.0), (ny - 1, north, -1.0)):
            wind = jnp.maximum(sign * jnp.broadcast_to(wn[x][:, y : y + 1], (nz, LANES)), 0.0)
            at = pl.ds(pl.multiple_of((x * ny + y) * nz, nz), nz)
            came = halo[x].astype(F32)
            for h in range(halves):
                adv[h, at, :] = adv[h, at, :] + wind * came[h * nz : (h + 1) * nz]
        return carry

    lax.fori_loop(0, nx, edges, 0, unroll=4)

    for send, x, halo, sign in ((sends[2], 0, west, 1.0), (sends[3], nx - 1, east, -1.0)):
        send.wait_recv()
        wind = jnp.maximum(sign * we[x], 0.0)
        for y in range(ny):
            at = pl.ds((x * ny + y) * nz, nz)
            spread_wind = jnp.broadcast_to(wind[:, y : y + 1], (nz, LANES))
            came = halo[y].astype(F32)
            for h in range(halves):
                adv[h, at, :] = adv[h, at, :] + spread_wind * came[h * nz : (h + 1) * nz]

    collide_all()

    rim = edge_flux.shape[0]
    order = lax.broadcasted_iota(I32, (rim, LANES), 0)
    near = jnp.where(order < ny, order, order - ny + (nx - 1) * ny)
    far = order - 2 * ny
    side = jnp.where(far < nx, far * ny, (far - nx) * ny + ny - 1)
    extra[0:rim, :] = collected(jnp.where(order < 2 * ny, near, side))
    for g in range(rim // 8):
        r = g * 8
        if r < 2 * ny:
            x, y = (0, r) if r < ny else (nx - 1, r - ny)
            base, stride = (x * ny + y) * nz, nz
        else:
            x, y = (r - 2 * ny, 0) if r - 2 * ny < nx else (r - 2 * ny - nx, ny - 1)
            base, stride = (x * ny + y) * nz, ny * nz
        for h in range(halves):
            lanes = slice(h * LANES, (h + 1) * LANES)
            extra[r : r + 8, lanes] = extra[r : r + 8, lanes] + drained(base, stride, lanes, h)
    edge_flux[...] = extra[0:rim, :].astype(BF16)

    @pl.when(me == top)
    def _():
        down(inner).start()
        arrived[...] = jnp.zeros(arrived.shape, BF16)
        edge_in[...] = jnp.zeros(edge_in.shape, BF16)

    @pl.when(me == top - 1)
    def _():
        relay(inner)

    @pl.when(me < top - 1)
    def _():
        for p in range(inner + 1):
            relay(p)

    @pl.when(me > 0)
    def _():
        for p in range(inner + 1):
            down(p).wait_send()

    for send in sends:
        send.wait_send()


def settle_kernel(
    adv_in, moist, arrived, edge_in, cells, target, fall, adv, out, flow, inverse, level_out, staged, out_sem
):
    nx, ny, packed, _ = out.shape
    nz, bins = fall.shape
    halves = bins // LANES
    width, blocks = cells.shape
    plane = target.shape[0] * target.shape[1]
    gx, gy = lax.axis_index("gx"), lax.axis_index("gy")

    inverse[...] = 1.0 / (1.0 + fall[...])
    flow[...] = arrived[...].astype(F32)
    rim = edge_in[...].astype(F32)
    flow[0:ny, :] = rim[0:ny]
    flow[(nx - 1) * ny : nx * ny, :] = rim[ny : 2 * ny]
    for i in range(nx):
        flow[i * ny : i * ny + 1, :] = rim[2 * ny + i : 2 * ny + i + 1]
        flow[i * ny + ny - 1 : i * ny + ny, :] = rim[2 * ny + nx + i : 2 * ny + nx + i + 1]

    def scatter(k, carry):
        @pl.when(target[gx, gy, 0, k] < plane)
        def _():
            for j in range(width):
                cell = pl.ds(cells[j, k], 1)
                for h in range(halves):
                    adv[h, cell, :] = moist[h, pl.ds(j * blocks + k, 1), :]

        return carry

    lax.fori_loop(0, blocks, scatter, 0)

    def push(x, slot):
        return pltpu.make_async_copy(staged.at[slot], out.at[x], out_sem.at[slot])

    slots = staged.shape[0]

    def row(x, carry):
        slot = lax.rem(x, slots)
        for g in range(ny // 8):
            base = pl.multiple_of((x * ny + g * 8) * nz, 8 * nz)
            at = pl.ds(pl.multiple_of(x * ny + g * 8, 8), 8)
            for h in range(halves):
                lanes = slice(h * LANES, (h + 1) * LANES)
                inflow = flow[at, lanes]
                for z in reversed(range(nz)):
                    level = adv[h, pl.ds(base + z, 8, stride=nz), :]
                    value = (level + inflow) * inverse[z : z + 1, lanes]
                    level_out[h, pl.ds(g * 8 * nz + z, 8, stride=nz), :] = value
                    inflow = value * fall[z : z + 1, lanes]

        @pl.when(x >= slots)
        def _():
            push(x - slots, slot).wait()

        for y in range(ny):
            pieces = [level_out[h, y * nz : (y + 1) * nz, :] for h in range(halves)]
            staged[slot, y] = jnp.concatenate(pieces, axis=0).astype(BF16)
        push(x, slot).start()
        return carry

    lax.fori_loop(0, nx, row, 0)
    for x in range(nx - slots, nx):
        push(x, x % slots).wait()


def body(
    spectrum,
    wind_east,
    wind_north,
    fall_rate,
    cloud_cells,
    block_target,
    pair_inputs,
    pair_outputs,
    loss_kernel,
    fragments,
):
    nx, ny, nz, bins = spectrum.shape
    halves = bins // LANES
    cells = nx * ny * nz
    columns = nx * ny
    blocks, width = cloud_cells.shape[3], cloud_cells.shape[4]
    total = blocks * width
    pairs = pair_outputs.shape[0]
    packed = nz * halves
    winds = (wind_east.transpose(0, 2, 1), wind_north.transpose(0, 2, 1))
    listed = cloud_cells.reshape(blocks, width).T
    dma = pltpu.SemaphoreType.DMA
    hbm = pl.BlockSpec(memory_space=pltpu.HBM)
    smem = pl.BlockSpec(memory_space=pltpu.SMEM)
    vmem = pl.BlockSpec(memory_space=pltpu.VMEM)
    dense = spectrum.reshape(nx, ny, nz, halves, LANES).transpose(0, 1, 3, 2, 4).reshape(nx, ny, packed, LANES)
    span = max(s for s in range(1, 7) if (nx - 2) % s == 0)
    inner = (nx - 2) // span
    rim = 2 * (nx + ny)
    parts = 4

    adv, moist, arrived, edge_in = pl.pallas_call(
        step_kernel,
        out_shape=(
            pltpu.VMEM((halves, cells, LANES), F32),
            pltpu.VMEM((halves, total, LANES), F32),
            pltpu.VMEM((columns, bins), BF16),
            pltpu.VMEM((rim, bins), BF16),
        ),
        in_specs=[hbm] * 10,
        out_specs=(vmem,) * 4,
        scratch_shapes=[
            pltpu.VMEM((nx + 2, ny, packed, LANES), BF16),
            pltpu.VMEM(winds[0].shape, F32),
            pltpu.VMEM(winds[1].shape, F32),
            pltpu.VMEM((ny, packed, LANES), BF16),
            pltpu.VMEM((ny, packed, LANES), BF16),
            pltpu.VMEM((nx, packed, LANES), BF16),
            pltpu.VMEM((nx, packed, LANES), BF16),
            pltpu.VMEM(fall_rate.shape, F32),
            pltpu.SMEM((width, blocks), I32),
            pltpu.VMEM((width, blocks), I32),
            pltpu.VMEM(block_target.shape, I32),
            pltpu.VMEM(pair_inputs.shape, BF16),
            pltpu.VMEM(pair_outputs.shape, BF16),
            pltpu.VMEM(loss_kernel.shape, BF16),
            pltpu.VMEM(fragments.shape, BF16),
            pltpu.VMEM((halves, total, LANES), F32),
            pltpu.VMEM((total, bins), BF16),
            pltpu.VMEM((total, bins), F32),
            pltpu.VMEM((max(total // LANES, 8), LANES), I32),
            pltpu.VMEM((2 * nz, bins), F32),
            pltpu.VMEM(((nx - 2) * ny, bins), BF16),
            pltpu.VMEM((rim, bins), BF16),
            pltpu.VMEM((max(span * ny, rim), bins), F32),
            dma((parts,)),
            dma((10,)),
            dma((4,)),
            dma((4,)),
            dma((inner + 1,)),
            dma((inner + 1,)),
        ],
        compiler_params=pltpu.CompilerParams(
            collective_id=0, has_side_effects=True, vmem_limit_bytes=(60 << 20) - cells * bins * 4
        ),
        name="step",
    )(dense, *winds, fall_rate, listed, block_target, pair_inputs, pair_outputs, loss_kernel, fragments)

    slots = 4
    _, settled = pl.pallas_call(
        settle_kernel,
        out_shape=(
            pltpu.VMEM((halves, cells, LANES), F32),
            jax.ShapeDtypeStruct((nx, ny, packed, LANES), BF16),
        ),
        in_specs=[vmem] * 4 + [smem, smem, vmem],
        out_specs=(vmem, hbm),
        scratch_shapes=[
            pltpu.VMEM((columns, bins), F32),
            pltpu.VMEM((nz, bins), F32),
            pltpu.VMEM((halves, ny * nz, LANES), F32),
            pltpu.VMEM((slots, ny, packed, LANES), BF16),
            dma((slots,)),
        ],
        input_output_aliases={0: 0},
        compiler_params=pltpu.CompilerParams(vmem_limit_bytes=32 << 20),
        name="settle",
    )(adv, moist, arrived, edge_in, listed, block_target, fall_rate)
    return settled.reshape(nx, ny, halves, nz, LANES).transpose(0, 1, 3, 2, 4).reshape(nx, ny, nz, bins)


def solution(mesh):
    in_specs = (
        P("gx", "gy", "gz", None),
        P("gx", "gy", "gz"),
        P("gx", "gy", "gz"),
        P("gz", None),
        P("gx", "gy", "gz", None, None),
        P(None, None, "gz", None),
        P(),
        P(),
        P(),
        P(),
    )
    out_specs = P("gx", "gy", "gz", None)
    return jax.shard_map(body, mesh=mesh, in_specs=in_specs, out_specs=out_specs, check_vma=False)
```

profile of v0, /device:TPU:0, one launch (start us, length us, event | category | flops | bytes accessed | tf_op | source)
XLA Modules:
  0.0 40.3 jit_solution(12522773581527670603)
XLA Ops:
  0.0 30.5 %step.1 = (f32[2,8192,128]{2,1,0:T(8,128)S(1)}, f32[2,1024,128]{2,1,0:T(8,128)S(1)}, bf16[1024,256]{1,0:T(8,128)(2,1)S(1)}, bf16[128,256]{1,0:T(8,128)(2,1)S(1)}) custom-call(bf16[32,32,16,128]{3,2,1,0:T(8,128)(2,1)} %bitcast.17, f32[32,8,32]{2,1,0:T(8,128)} %bitcast.18, f32[32,8,32]{2,1,0:T(8,128)} %bitcast.19, f32[8,256]{1,0:T(8,128)} %fall.1, ...), custom_call_target="tpu_custom_call" | custom-call | tf_op jit(solution)/shard_map/step/pallas_call | solution.py:418
  30.5 0.0 copy-start
  30.5 0.7 %copy-done = f32[8,256]{1,0:T(8,128)S(1)} copy-done((f32[8,256]{1,0:T(8,128)S(1)}, f32[8,256]{1,0:T(8,128)}, u32[]{:S(2)}) %copy-start) | copy-done | bytes 8216
  31.2 0.0 copy-start.1
  31.2 0.7 %copy-done.1 = s32[1,1,1,64,16]{3,4,2,1,0:T(8,128)S(1)} copy-done((s32[1,1,1,64,16]{3,4,2,1,0:T(8,128)S(1)}, s32[1,1,1,64,16]{3,4,2,1,0:T(8,128)}, u32[]{:S(2)}) %copy-start.1) | copy-done | bytes 4120
  31.9 0.0 copy-start.2
  31.9 0.7 %copy-done.2 = s32[2,4,1,64]{3,2,1,0:T(1,128)S(1)} copy-done((s32[2,4,1,64]{3,2,1,0:T(1,128)S(1)}, s32[2,4,1,64]{3,2,1,0:T(1,128)}, u32[]{:S(2)}) %copy-start.2) | copy-done | bytes 2072
  32.6 7.7 %settle.1 = (f32[2,8192,128]{2,1,0:T(8,128)S(1)}, bf16[32,32,16,128]{3,2,1,0:T(8,128)(2,1)}) custom-call(f32[2,8192,128]{2,1,0:T(8,128)S(1)} %get-tuple-element.10.adv_in, f32[2,1024,128]{2,1,0:T(8,128)S(1)} %get-tuple-element.11.moist, bf16[1024,256]{1,0:T(8,128)(2,1)S(1)} %get-tuple-element.12.arrived, ...), custom_call_target="tpu_custom_call", output_to_operand_aliasing={{0}: (0, {})} | custom-call | tf_op jit(solution)/shard_map/settle/pallas_call | solution.py:466
Async XLA Ops:
  30.5 0.7 %copy-start = (f32[8,256]{1,0:T(8,128)S(1)}, f32[8,256]{1,0:T(8,128)}, u32[]{:S(2)}) copy-start(f32[8,256]{1,0:T(8,128)} %fall.1) | copy-start | bytes 24580
  31.2 0.7 %copy-start.1 = (s32[1,1,1,64,16]{3,4,2,1,0:T(8,128)S(1)}, s32[1,1,1,64,16]{3,4,2,1,0:T(8,128)}, u32[]{:S(2)}) copy-start(s32[1,1,1,64,16]{3,4,2,1,0:T(8,128)} %param.14) | copy-start | bytes 12292
  31.9 0.7 %copy-start.2 = (s32[2,4,1,64]{3,2,1,0:T(1,128)S(1)}, s32[2,4,1,64]{3,2,1,0:T(1,128)}, u32[]{:S(2)}) copy-start(s32[2,4,1,64]{3,2,1,0:T(1,128)} %target.1) | copy-start | bytes 6148
where the time goes:
time: 40.8 us; the launch traced here: 40.3 us
  Pallas kernels  38.2 us (94%)
  local copies, waits for them, and re-layouts  2.07 us (5%)
    pallas_call x1, Pallas kernels, body(): pl.pallas_call(step_kernel, out_shape=(pltpu.VMEM((halves, cells, LANES),...  30.5 us
    pallas_call x1, Pallas kernels, body(): pl.pallas_call(settle_kernel, out_shape=(pltpu.VMEM((halves, cells, LANES...  7.69 us
    unnamed x6, local copies, waits for them, and re-layouts  2.07 us

commit v1 on v0

v1 whole, which is shorter than its diff:
```python
import functools

import jax
import jax.numpy as jnp
from jax import lax
from jax.experimental import pallas as pl
from jax.experimental.pallas import tpu as pltpu
from jax.sharding import PartitionSpec as P

MESH = pl.DeviceIdType.MESH
F32 = jnp.float32
BF16 = jnp.bfloat16
I32 = jnp.int32
LANES = 128
GROUP = 8


def spot_of(column, level, levels):
    return (column // GROUP * levels + level) * GROUP + column % GROUP


def step_kernel(
    spec, winds_e, winds_n, fall_h, cells_h, target_h, pair_in_h, pair_out_h, loss_h, frag_h,
    adv, moist, arrived, edge_in, spots, fall,
    local, we, wn, west, east, south, north, cells, listed_v, target, pair_in, pair_out, loss, frag,
    rows, q, pz, ids, live, shares, settled, flux, edge_flux, extra,
    load_sem, in_sem, spot_sem, send_sem, recv_sem, down_sem, got_sem,
):
    nx, ny, packed, _ = spec.shape
    nz, bins = fall.shape
    halves = bins // LANES
    width, blocks = cells.shape
    total = width * blocks
    pairs = pair_out.shape[0]
    parts = load_sem.shape[0]
    per = nx // parts
    gx, gy, me = lax.axis_index("gx"), lax.axis_index("gy"), lax.axis_index("gz")
    sx, sy, count = lax.axis_size("gx"), lax.axis_size("gy"), lax.axis_size("gz")
    plane = sx * sy
    top = count - 1
    to_west = {"gx": lax.rem(gx + sx - 1, sx)}
    to_east = {"gx": lax.rem(gx + 1, sx)}
    to_south = {"gy": lax.rem(gy + sy - 1, sy)}
    to_north = {"gy": lax.rem(gy + 1, sy)}
    above = {"gz": lax.rem(me + 1, count)}
    below = {"gz": lax.rem(me + top, count)}

    barrier = pltpu.get_barrier_semaphore()
    for peer in (to_west, to_east, to_south, to_north, above, below):
        pl.semaphore_signal(barrier, inc=1, device_id=peer, device_id_type=MESH)

    def fetch(i, src, dst):
        return pltpu.make_async_copy(src, dst, in_sem.at[i])

    wind_loads = [fetch(0, winds_e, we), fetch(1, winds_n, wn)]
    loads = [
        pltpu.make_async_copy(spec.at[pl.ds(p * per, per)], local.at[pl.ds(1 + p * per, per)], load_sem.at[p])
        for p in range(parts)
    ]
    small = [fetch(2, fall_h, fall), fetch(3, cells_h, listed_v), fetch(4, target_h, target)]
    weights = [
        fetch(6, pair_in_h, pair_in), fetch(7, pair_out_h, pair_out), fetch(8, loss_h, loss), fetch(9, frag_h, frag)
    ]
    for load in wind_loads + loads + small + weights:
        load.start()
    pl.semaphore_wait(barrier, 6)

    sends = [
        pltpu.make_async_remote_copy(
            src_ref=src,
            dst_ref=dst,
            send_sem=send_sem.at[i],
            recv_sem=recv_sem.at[i],
            device_id=peer,
            device_id_type=MESH,
        )
        for i, (src, dst, peer) in enumerate(
            (
                (spec.at[:, ny - 1], south, to_north),
                (spec.at[:, 0], north, to_south),
                (spec.at[nx - 1], west, to_east),
                (spec.at[0], east, to_west),
            )
        )
    ]
    for send in sends:
        send.start()

    zero_row = jnp.zeros((ny, packed, LANES), BF16)
    local[0] = zero_row
    local[nx + 1] = zero_row

    def stacked(tile):
        return jnp.concatenate([tile] * halves, axis=0).astype(BF16)

    def spread(tile, y):
        return jnp.broadcast_to(tile[:, y : y + 1], (packed, LANES))

    def one_row(x, carry):
        east_w, north_w = stacked(we[x]), stacked(wn[x])
        zero = jnp.zeros((packed, LANES), BF16)
        behind = zero
        centre = local[x + 1, 0]
        for y in range(ny):
            ahead = local[x + 1, y + 1] if y + 1 < ny else zero
            a, b = spread(east_w, y), spread(north_w, y)
            up_x = jnp.where(a > 0, local[x, y], local[x + 2, y])
            up_y = jnp.where(b > 0, behind, ahead)
            change = jnp.abs(a) * (up_x - centre) + jnp.abs(b) * (up_y - centre)
            value = centre.astype(F32) + change.astype(F32)
            base = pl.multiple_of((x * ny + y - y % GROUP) * nz, GROUP * nz)
            for h in range(halves):
                adv[h, pl.ds(base + y % GROUP, nz, stride=GROUP), :] = value[h * nz : (h + 1) * nz]
            behind, centre = centre, ahead
        return carry

    for load in small:
        load.wait()

    ratio = fall[...] / (1.0 + fall[...])
    share = jnp.ones((1, bins), F32)
    for z in range(nz):
        share = share * ratio[z : z + 1, :]
        shares[z : z + 1, :] = share
    shares[nz : 2 * nz, :] = ratio
    gain = share

    listed = listed_v[...]
    spots[...] = spot_of(listed // nz, listed % nz, nz)
    spot = pltpu.make_async_copy(spots, cells, spot_sem.at[0])
    spot.start()
    cloudy = target[gx, gy] < plane
    columns = jnp.where(cloudy, listed // nz, -1)
    per_tile = LANES // blocks
    for t in range(total // LANES):
        ids[t : t + 1, :] = jnp.concatenate(
            [columns[t * per_tile + i : t * per_tile + i + 1, :] for i in range(per_tile)], axis=1
        )
    flags = jnp.broadcast_to(jnp.where(cloudy, 1.0, 0.0), (8, blocks)).T
    live[...] = jnp.broadcast_to(flags[:, 0:1], (blocks, LANES))
    heights = (listed % nz).astype(F32).T
    high = shares[0:nz, :].astype(BF16)
    low = (shares[0:nz, :] - high.astype(F32)).astype(BF16)
    table = jnp.concatenate([high, low, jnp.zeros((LANES - 2 * nz, bins), BF16)], axis=0)
    lane = lax.broadcasted_iota(I32, (blocks, LANES), 1)
    level_of = jnp.where(lane < 2 * nz, lane % nz, -1).astype(F32)
    picks = [
        jnp.where(jnp.broadcast_to(heights[:, j : j + 1], (blocks, LANES)) == level_of, 1.0, 0.0).astype(BF16)
        for j in range(width)
    ]
    pz[...] = jnp.dot(jnp.concatenate(picks, axis=0), table, preferred_element_type=F32)
    for load in wind_loads:
        load.wait()
    done = 0
    for p in range(parts):
        loads[p].wait()
        upto = nx if p == parts - 1 else (p + 1) * per - 1
        lax.fori_loop(done, upto, one_row, 0)
        done = upto

    for load in weights:
        load.wait()

    size = min(256, total)
    tile = min(256, pairs)
    inner = down_sem.shape[0] - 1
    span = (nx - 2) // inner
    wide = span * ny

    def gather(i):
        for r in range(i * size, (i + 1) * size):
            cell = pl.ds(cells[r // blocks, r % blocks], 1)
            for h in range(halves):
                rows[h, r : r + 1, :] = adv[h, cell, :]

    def collide(i):
        at = slice(i * size, (i + 1) * size)
        full = jnp.concatenate([rows[h, at, :] for h in range(halves)], axis=1)
        row = full.astype(BF16)
        decline = jnp.dot(row, loss[...], preferred_element_type=F32)
        losses = row.astype(F32) * decline
        gained = jnp.dot(losses.astype(BF16), frag[...], preferred_element_type=F32)
        for n in range(0, pairs, tile):
            first = jnp.dot(row, pair_in[:, n : n + tile], preferred_element_type=F32)
            second = jnp.dot(row, pair_in[:, pairs + n : pairs + n + tile], preferred_element_type=F32)
            product = (first * second).astype(BF16)
            gained = gained + jnp.dot(product, pair_out[n : n + tile, :], preferred_element_type=F32)
        tendency = (gained - losses).astype(BF16).astype(F32)
        alive = jnp.concatenate([jnp.concatenate([live[...]] * halves, axis=1)] * (size // blocks), axis=0)
        tendency = jnp.where(alive > 0.0, tendency, 0.0)
        q[at, :] = (tendency * pz[at, :]).astype(BF16)
        after = full + tendency
        for h in range(halves):
            moist[h, at, :] = after[:, h * LANES : (h + 1) * LANES]

    def total_of(terms):
        while len(terms) > 1:
            terms = [a + b for a, b in zip(terms[::2], terms[1::2])]
        return terms[0]

    def sink(x):
        for g in range(x * ny // GROUP, (x + 1) * ny // GROUP):
            at = slice(g * GROUP - ny, (g + 1) * GROUP - ny)
            for h in range(halves):
                lanes = slice(h * LANES, (h + 1) * LANES)
                terms = [
                    adv[h, (g * nz + z) * GROUP : (g * nz + z + 1) * GROUP, :] * shares[z : z + 1, lanes]
                    for z in range(nz)
                ]
                settled[at, lanes] = total_of(terms)

    def collide_all(also):
        chunks = total // size
        gather(0)
        for i in range(chunks):
            if i + 1 < chunks:
                gather(i + 1)
            if also:
                for x in range(1 + i * (nx - 2) // chunks, 1 + (i + 1) * (nx - 2) // chunks):
                    sink(x)
            collide(i)

    def collected(column):
        hot = [
            jnp.where(jnp.broadcast_to(ids[t : t + 1, :], column.shape) == column, 1.0, 0.0).astype(BF16)
            for t in range(total // LANES)
        ]
        return jnp.dot(jnp.concatenate(hot, axis=1), q[...], preferred_element_type=F32)

    def drained(column, apart, lanes, h):
        first = spot_of(column, 0, nz)
        stride = 1 if apart == 1 else apart * nz
        terms = [
            adv[h, pl.ds(first + z * GROUP, GROUP, stride=stride), :] * shares[z : z + 1, lanes] for z in range(nz)
        ]
        return total_of(terms)

    def down(p):
        src = edge_flux if p == inner else flux.at[pl.ds(p * wide, wide)]
        dst = edge_in if p == inner else arrived.at[pl.ds((1 + p * span) * ny, wide)]
        return pltpu.make_async_remote_copy(
            src_ref=src,
            dst_ref=dst,
            send_sem=down_sem.at[p],
            recv_sem=got_sem.at[p],
            device_id={"gz": jnp.maximum(me - 1, 0)},
            device_id_type=MESH,
        )

    def relay(p):
        down(p).wait_recv()

        @pl.when(me > 0)
        def _():
            if p == inner:
                edge_flux[...] = (edge_flux[...].astype(F32) + edge_in[...].astype(F32) * gain).astype(BF16)
            else:
                at = pl.ds(p * wide, wide)
                got = arrived[pl.ds((1 + p * span) * ny, wide), :].astype(F32)
                flux[at, :] = (flux[at, :].astype(F32) + got * gain).astype(BF16)
            down(p).start()

    spot.wait()
    collide_all(True)

    for p in range(inner):
        column = lax.broadcasted_iota(I32, (wide, LANES), 0) + (1 + p * span) * ny
        at = slice(p * wide, (p + 1) * wide)
        flux[at, :] = (collected(column) + settled[at, :]).astype(BF16)

        @pl.when(me == top)
        def _():
            down(p).start()

        @pl.when(me == top - 1)
        def _():
            relay(p)

    for send in sends[:2]:
        send.wait_recv()

    def add_halo(column, wind, halo):
        came = wind.astype(F32) * halo.astype(F32)
        at = pl.ds(spot_of(column, 0, nz), nz, stride=GROUP)
        for h in range(halves):
            adv[h, at, :] = adv[h, at, :] + came[h * nz : (h + 1) * nz]

    def edges(x, carry):
        winds = stacked(wn[x])
        add_halo(x * ny, jnp.maximum(spread(winds, 0), 0), south[x])
        add_halo(x * ny + ny - 1, jnp.maximum(-spread(winds, ny - 1), 0), north[x])
        return carry

    lax.fori_loop(0, nx, edges, 0, unroll=8)

    for send, x, halo, sign in ((sends[2], 0, west, 1.0), (sends[3], nx - 1, east, -1.0)):
        send.wait_recv()
        winds = jnp.maximum(sign * stacked(we[x]), 0)
        for y in range(ny):
            add_halo(x * ny + y, spread(winds, y), halo[y])

    collide_all(False)

    rim = edge_flux.shape[0]
    order = lax.broadcasted_iota(I32, (rim, LANES), 0)
    near = jnp.where(order < ny, order, order - ny + (nx - 1) * ny)
    far = order - 2 * ny
    side = jnp.where(far < nx, far * ny, (far - nx) * ny + ny - 1)
    extra[0:rim, :] = collected(jnp.where(order < 2 * ny, near, side))
    for r in range(0, rim, GROUP):
        if r < 2 * ny:
            x, y = (0, r) if r < ny else (nx - 1, r - ny)
            base, stride = x * ny + y, 1
        else:
            x, y = (r - 2 * ny, 0) if r - 2 * ny < nx else (r - 2 * ny - nx, ny - 1)
            base, stride = x * ny + y, ny
        for h in range(halves):
            lanes = slice(h * LANES, (h + 1) * LANES)
            extra[r : r + GROUP, lanes] = extra[r : r + GROUP, lanes] + drained(base, stride, lanes, h)
    edge_flux[...] = extra[0:rim, :].astype(BF16)

    @pl.when(me == top)
    def _():
        down(inner).start()
        arrived[...] = jnp.zeros(arrived.shape, BF16)
        edge_in[...] = jnp.zeros(edge_in.shape, BF16)

    @pl.when(me == top - 1)
    def _():
        relay(inner)

    @pl.when(me < top - 1)
    def _():
        for p in range(inner + 1):
            relay(p)

    @pl.when(me > 0)
    def _():
        for p in range(inner + 1):
            down(p).wait_send()

    for send in sends:
        send.wait_send()


def settle_kernel(
    adv_in, moist, arrived, edge_in, spots, fall, adv, out, cells, flow, inverse, ratio, level_out, staged,
    cell_sem, out_sem
):
    nx, ny, packed, _ = out.shape
    nz, bins = fall.shape
    halves = bins // LANES
    width, blocks = cells.shape
    slots = level_out.shape[0]

    fetch = pltpu.make_async_copy(spots, cells, cell_sem.at[0])
    fetch.start()
    inverse[...] = 1.0 / (1.0 + fall[...])
    ratio[...] = fall[...] * inverse[...]
    flow[...] = arrived[...].astype(F32)
    rim = edge_in[...].astype(F32)
    flow[0:ny, :] = rim[0:ny]
    flow[(nx - 1) * ny : nx * ny, :] = rim[ny : 2 * ny]
    for i in range(nx):
        flow[i * ny : i * ny + 1, :] = rim[2 * ny + i : 2 * ny + i + 1]
        flow[i * ny + ny - 1 : i * ny + ny, :] = rim[2 * ny + nx + i : 2 * ny + nx + i + 1]
    fetch.wait()

    def scatter(j, carry):
        for k in range(blocks):
            cell = pl.ds(cells[j, k], 1)
            for h in range(halves):
                adv[h, cell, :] = moist[h, pl.ds(j * blocks + k, 1), :]
        return carry

    lax.fori_loop(0, width, scatter, 0)

    def push(i):
        at = pl.ds(i * slots, slots)
        return pltpu.make_async_copy(staged.at[at], out.at[at], out_sem.at[i])

    def some_rows(i, carry):
        for slot in range(slots):
            x = i * slots + slot
            for g in range(ny // GROUP):
                column = pl.multiple_of(x * ny + g * GROUP, GROUP)
                for h in range(halves):
                    lanes = slice(h * LANES, (h + 1) * LANES)
                    inflow = flow[pl.ds(column, GROUP), lanes]
                    for z in reversed(range(nz)):
                        held = adv[h, pl.ds(pl.multiple_of(column * nz + z * GROUP, GROUP), GROUP), :] + inflow
                        to = pl.ds(g * GROUP * nz + z, GROUP, stride=nz)
                        level_out[slot, h, to, :] = held * inverse[z : z + 1, lanes]
                        inflow = held * ratio[z : z + 1, lanes]
            for y in range(ny):
                pieces = [level_out[slot, h, y * nz : (y + 1) * nz, :] for h in range(halves)]
                staged[x, y] = jnp.concatenate(pieces, axis=0).astype(BF16)
        push(i).start()
        return carry

    lax.fori_loop(0, nx // slots, some_rows, 0)
    for i in range(nx // slots):
        push(i).wait()


def body(
    spectrum,
    wind_east,
    wind_north,
    fall_rate,
    cloud_cells,
    block_target,
    pair_inputs,
    pair_outputs,
    loss_kernel,
    fragments,
):
    nx, ny, nz, bins = spectrum.shape
    halves = bins // LANES
    cells = nx * ny * nz
    columns = nx * ny
    blocks, width = cloud_cells.shape[3], cloud_cells.shape[4]
    total = blocks * width
    pairs = pair_outputs.shape[0]
    packed = nz * halves
    winds = (wind_east.transpose(0, 2, 1), wind_north.transpose(0, 2, 1))
    listed = cloud_cells.reshape(blocks, width).T
    dma = pltpu.SemaphoreType.DMA
    hbm = pl.BlockSpec(memory_space=pltpu.HBM)
    vmem = pl.BlockSpec(memory_space=pltpu.VMEM)
    dense = spectrum.reshape(nx, ny, nz, halves, LANES).transpose(0, 1, 3, 2, 4).reshape(nx, ny, packed, LANES)
    span = max(s for s in range(1, 11) if (nx - 2) % s == 0)
    inner = (nx - 2) // span
    rim = 2 * (nx + ny)
    parts = 4

    adv, moist, arrived, edge_in, spots, fall_v = pl.pallas_call(
        step_kernel,
        out_shape=(
            pltpu.VMEM((halves, cells, LANES), F32),
            pltpu.VMEM((halves, total, LANES), F32),
            pltpu.VMEM((columns, bins), BF16),
            pltpu.VMEM((rim, bins), BF16),
            pltpu.VMEM((width, blocks), I32),
            pltpu.VMEM(fall_rate.shape, F32),
        ),
        in_specs=[hbm] * 10,
        out_specs=(vmem,) * 6,
        scratch_shapes=[
            pltpu.VMEM((nx + 2, ny, packed, LANES), BF16),
            pltpu.VMEM(winds[0].shape, F32),
            pltpu.VMEM(winds[1].shape, F32),
            pltpu.VMEM((ny, packed, LANES), BF16),
            pltpu.VMEM((ny, packed, LANES), BF16),
            pltpu.VMEM((nx, packed, LANES), BF16),
            pltpu.VMEM((nx, packed, LANES), BF16),
            pltpu.SMEM((width, blocks), I32),
            pltpu.VMEM((width, blocks), I32),
            pltpu.VMEM(block_target.shape, I32),
            pltpu.VMEM(pair_inputs.shape, BF16),
            pltpu.VMEM(pair_outputs.shape, BF16),
            pltpu.VMEM(loss_kernel.shape, BF16),
            pltpu.VMEM(fragments.shape, BF16),
            pltpu.VMEM((halves, total, LANES), F32),
            pltpu.VMEM((total, bins), BF16),
            pltpu.VMEM((total, bins), F32),
            pltpu.VMEM((max(total // LANES, 8), LANES), I32),
            pltpu.VMEM((blocks, LANES), F32),
            pltpu.VMEM((2 * nz, bins), F32),
            pltpu.VMEM(((nx - 2) * ny, bins), F32),
            pltpu.VMEM(((nx - 2) * ny, bins), BF16),
            pltpu.VMEM((rim, bins), BF16),
            pltpu.VMEM((rim, bins), F32),
            dma((parts,)),
            dma((10,)),
            dma((1,)),
            dma((4,)),
            dma((4,)),
            dma((inner + 1,)),
            dma((inner + 1,)),
        ],
        compiler_params=pltpu.CompilerParams(
            collective_id=0, has_side_effects=True, vmem_limit_bytes=(60 << 20) - cells * bins * 4
        ),
        name="step",
    )(dense, *winds, fall_rate, listed, block_target, pair_inputs, pair_outputs, loss_kernel, fragments)

    slots = 4
    _, settled = pl.pallas_call(
        settle_kernel,
        out_shape=(
            pltpu.VMEM((halves, cells, LANES), F32),
            jax.ShapeDtypeStruct((nx, ny, packed, LANES), BF16),
        ),
        in_specs=[vmem] * 6,
        out_specs=(vmem, hbm),
        scratch_shapes=[
            pltpu.SMEM((width, blocks), I32),
            pltpu.VMEM((columns, bins), F32),
            pltpu.VMEM((nz, bins), F32),
            pltpu.VMEM((nz, bins), F32),
            pltpu.VMEM((slots, halves, ny * nz, LANES), F32),
            pltpu.VMEM((nx, ny, packed, LANES), BF16),
            dma((1,)),
            dma((nx // slots,)),
        ],
        input_output_aliases={0: 0},
        compiler_params=pltpu.CompilerParams(vmem_limit_bytes=32 << 20),
        name="settle",
    )(adv, moist, arrived, edge_in, spots, fall_v)
    return settled.reshape(nx, ny, halves, nz, LANES).transpose(0, 1, 3, 2, 4).reshape(nx, ny, nz, bins)


def solution(mesh):
    in_specs = (
        P("gx", "gy", "gz", None),
        P("gx", "gy", "gz"),
        P("gx", "gy", "gz"),
        P("gz", None),
        P("gx", "gy", "gz", None, None),
        P(None, None, "gz", None),
        P(),
        P(),
        P(),
        P(),
    )
    out_specs = P("gx", "gy", "gz", None)
    return jax.shard_map(body, mesh=mesh, in_specs=in_specs, out_specs=out_specs, check_vma=False)
```

time: 40.8 us -> 31 us (0.76); the launches traced: 40.3 us -> 30.9 us
  Pallas kernels: 38.2 us -> 30.9 us
  local copies, waits for them, and re-layouts: 2.07 us -> 0 us
    pallas_call x1, Pallas kernels: 30.5 us -> 26.5 us  [body(): pl.pallas_call(step_kernel, out_shape=(pltpu.VMEM((halves, cells, LANES),...]
    pallas_call x1, Pallas kernels: 7.69 us -> 4.37 us  [body(): pl.pallas_call(settle_kernel, out_shape=(pltpu.VMEM((halves, cells, LANES...]
    unnamed x6 -> x0, local copies, waits for them, and re-layouts: 2.07 us -> none
where the time goes in v1:
time: 31 us; the launch traced here: 30.9 us
  Pallas kernels  30.9 us (100%)
    pallas_call x1, Pallas kernels, body(): pl.pallas_call(step_kernel, out_shape=(pltpu.VMEM((halves, cells, LANES),...  26.5 us
    pallas_call x1, Pallas kernels, body(): pl.pallas_call(settle_kernel, out_shape=(pltpu.VMEM((halves, cells, LANES...  4.37 us

profile of v1, /device:TPU:0, one launch (start us, length us, event | category | flops | bytes accessed | tf_op | source)
XLA Modules:
  0.0 30.9 jit_solution(2894870956140288383)
XLA Ops:
  0.0 26.5 %step.1 = (f32[2,8192,128]{2,1,0:T(8,128)S(1)}, f32[2,1024,128]{2,1,0:T(8,128)S(1)}, bf16[1024,256]{1,0:T(8,128)(2,1)S(1)}, bf16[128,256]{1,0:T(8,128)(2,1)S(1)}...) custom-call(bf16[32,32,16,128]{3,2,1,0:T(8,128)(2,1)} %bitcast.15, f32[32,8,32]{2,1,0:T(8,128)} %bitcast.16, ...), custom_call_target="tpu_custom_call" | custom-call | tf_op jit(solution)/shard_map/step/pallas_call | solution.py:437
  26.5 4.4 %settle.1 = (f32[2,8192,128]{2,1,0:T(8,128)S(1)}, bf16[32,32,16,128]{3,2,1,0:T(8,128)(2,1)}) custom-call(f32[2,8192,128]{2,1,0:T(8,128)S(1)} %get-tuple-element.12.adv_in, f32[2,1024,128]{2,1,0:T(8,128)S(1)} %get-tuple-element.13.moist, bf16[1024,256]{1,0:T(8,128)(2,1)S(1)} %get-tuple-element.14.arrived, ...), custom_call_target="tpu_custom_call", output_to_operand_aliasing={{0}: (0, {})} | custom-call | tf_op jit(solution)/shard_map/settle/pallas_call | solution.py:489

commit v2 on v1

--- a/solution.py
+++ b/solution.py
@@ -23,7 +23,7 @@
     spec, winds_e, winds_n, fall_h, cells_h, target_h, pair_in_h, pair_out_h, loss_h, frag_h,
     adv, moist, arrived, edge_in, spots, fall,
     local, we, wn, west, east, south, north, cells, listed_v, target, pair_in, pair_out, loss, frag,
-    rows, q, pz, ids, live, shares, settled, flux, edge_flux, extra,
+    rows, q, pz, ids, live, shares, picks, table, settled, flux, edge_flux, extra,
     load_sem, in_sem, spot_sem, send_sem, recv_sem, down_sem, got_sem,
 ):
     nx, ny, packed, _ = spec.shape
@@ -61,7 +61,7 @@
     weights = [
         fetch(6, pair_in_h, pair_in), fetch(7, pair_out_h, pair_out), fetch(8, loss_h, loss), fetch(9, frag_h, frag)
     ]
-    for load in wind_loads + loads + small + weights:
+    for load in small + wind_loads + loads + weights:
         load.start()
     pl.semaphore_wait(barrier, 6)
 
@@ -96,14 +96,41 @@
     def spread(tile, y):
         return jnp.broadcast_to(tile[:, y : y + 1], (packed, LANES))
 
-    def one_row(x, carry):
-        east_w, north_w = stacked(we[x]), stacked(wn[x])
+    def total_of(terms):
+        while len(terms) > 1:
+            terms = [a + b for a, b in zip(terms[::2], terms[1::2])]
+        return terms[0]
+
+    def sink(x):
+        for g in range(ny // GROUP):
+            at = pl.ds(pl.multiple_of(x * ny + g * GROUP, GROUP), GROUP)
+            base = pl.multiple_of((x * ny + g * GROUP) * nz, GROUP * nz)
+            for h in range(halves):
+                lanes = slice(h * LANES, (h + 1) * LANES)
+                terms = [adv[h, pl.ds(base + z * GROUP, GROUP), :] * shares[z : z + 1, lanes] for z in range(nz)]
+                settled[at, lanes] = total_of(terms)
+
+    share_rows = total // nx
+
+    def two_rows(i, carry):
+        for turn in range(2):
+            one_row(2 * i + turn)
+        return carry
+
+    def one_row(x):
+        both = jnp.concatenate([we[x]] * (halves // 2) + [wn[x]] * (halves // 2), axis=0).astype(BF16)
+        some = pl.ds(pl.multiple_of(x * share_rows, share_rows), share_rows)
+        pz[some, :] = jnp.dot(picks[some, :], table[...], preferred_element_type=F32)
+        sink(jnp.maximum(x - 1, 0))
+
         zero = jnp.zeros((packed, LANES), BF16)
         behind = zero
         centre = local[x + 1, 0]
         for y in range(ny):
             ahead = local[x + 1, y + 1] if y + 1 < ny else zero
-            a, b = spread(east_w, y), spread(north_w, y)
+            pair = spread(both, y)
+            a = jnp.concatenate([pair[0:nz]] * halves, axis=0)
+            b = jnp.concatenate([pair[nz : 2 * nz]] * halves, axis=0)
             up_x = jnp.where(a > 0, local[x, y], local[x + 2, y])
             up_y = jnp.where(b > 0, behind, ahead)
             change = jnp.abs(a) * (up_x - centre) + jnp.abs(b) * (up_y - centre)
@@ -112,7 +139,6 @@
             for h in range(halves):
                 adv[h, pl.ds(base + y % GROUP, nz, stride=GROUP), :] = value[h * nz : (h + 1) * nz]
             behind, centre = centre, ahead
-        return carry
 
     for load in small:
         load.wait()
@@ -141,27 +167,26 @@
     heights = (listed % nz).astype(F32).T
     high = shares[0:nz, :].astype(BF16)
     low = (shares[0:nz, :] - high.astype(F32)).astype(BF16)
-    table = jnp.concatenate([high, low, jnp.zeros((LANES - 2 * nz, bins), BF16)], axis=0)
+    table[...] = jnp.concatenate([high, low, jnp.zeros((LANES - 2 * nz, bins), BF16)], axis=0)
     lane = lax.broadcasted_iota(I32, (blocks, LANES), 1)
     level_of = jnp.where(lane < 2 * nz, lane % nz, -1).astype(F32)
-    picks = [
-        jnp.where(jnp.broadcast_to(heights[:, j : j + 1], (blocks, LANES)) == level_of, 1.0, 0.0).astype(BF16)
-        for j in range(width)
-    ]
-    pz[...] = jnp.dot(jnp.concatenate(picks, axis=0), table, preferred_element_type=F32)
+    for j in range(width):
+        hit = jnp.broadcast_to(heights[:, j : j + 1], (blocks, LANES)) == level_of
+        picks[j * blocks : (j + 1) * blocks, :] = jnp.where(hit, 1.0, 0.0).astype(BF16)
+
     for load in wind_loads:
         load.wait()
     done = 0
     for p in range(parts):
         loads[p].wait()
-        upto = nx if p == parts - 1 else (p + 1) * per - 1
-        lax.fori_loop(done, upto, one_row, 0)
+        upto = nx // 2 if p == parts - 1 else ((p + 1) * per - 1) // 2
+        lax.fori_loop(done, upto, two_rows, 0)
         done = upto
 
     for load in weights:
         load.wait()
 
-    size = min(256, total)
+    size = min(512, total)
     tile = min(256, pairs)
     inner = down_sem.shape[0] - 1
     span = (nx - 2) // inner
@@ -193,31 +218,12 @@
         for h in range(halves):
             moist[h, at, :] = after[:, h * LANES : (h + 1) * LANES]
 
-    def total_of(terms):
-        while len(terms) > 1:
-            terms = [a + b for a, b in zip(terms[::2], terms[1::2])]
-        return terms[0]
-
-    def sink(x):
-        for g in range(x * ny // GROUP, (x + 1) * ny // GROUP):
-            at = slice(g * GROUP - ny, (g + 1) * GROUP - ny)
-            for h in range(halves):
-                lanes = slice(h * LANES, (h + 1) * LANES)
-                terms = [
-                    adv[h, (g * nz + z) * GROUP : (g * nz + z + 1) * GROUP, :] * shares[z : z + 1, lanes]
-                    for z in range(nz)
-                ]
-                settled[at, lanes] = total_of(terms)
-
-    def collide_all(also):
+    def collide_all():
         chunks = total // size
         gather(0)
         for i in range(chunks):
             if i + 1 < chunks:
                 gather(i + 1)
-            if also:
-                for x in range(1 + i * (nx - 2) // chunks, 1 + (i + 1) * (nx - 2) // chunks):
-                    sink(x)
             collide(i)
 
     def collected(column):
@@ -261,12 +267,14 @@
             down(p).start()
 
     spot.wait()
-    collide_all(True)
+    collide_all()
 
     for p in range(inner):
         column = lax.broadcasted_iota(I32, (wide, LANES), 0) + (1 + p * span) * ny
-        at = slice(p * wide, (p + 1) * wide)
-        flux[at, :] = (collected(column) + settled[at, :]).astype(BF16)
+        held = settled[(1 + p * span) * ny : (1 + (p + 1) * span) * ny, :]
+        flux[p * wide : (p + 1) * wide, :] = (collected(column) + held).astype(BF16)
+
+    for p in range(inner):
 
         @pl.when(me == top)
         def _():
@@ -299,7 +307,7 @@
         for y in range(ny):
             add_halo(x * ny + y, spread(winds, y), halo[y])
 
-    collide_all(False)
+    collide_all()
 
     rim = edge_flux.shape[0]
     order = lax.broadcasted_iota(I32, (rim, LANES), 0)
@@ -366,14 +374,10 @@
         flow[i * ny + ny - 1 : i * ny + ny, :] = rim[2 * ny + nx + i : 2 * ny + nx + i + 1]
     fetch.wait()
 
-    def scatter(j, carry):
-        for k in range(blocks):
-            cell = pl.ds(cells[j, k], 1)
-            for h in range(halves):
-                adv[h, cell, :] = moist[h, pl.ds(j * blocks + k, 1), :]
-        return carry
-
-    lax.fori_loop(0, width, scatter, 0)
+    for r in range(width * blocks):
+        cell = pl.ds(cells[r // blocks, r % blocks], 1)
+        for h in range(halves):
+            adv[h, cell, :] = moist[h, r : r + 1, :]
 
     def push(i):
         at = pl.ds(i * slots, slots)
@@ -467,7 +471,9 @@
             pltpu.VMEM((max(total // LANES, 8), LANES), I32),
             pltpu.VMEM((blocks, LANES), F32),
             pltpu.VMEM((2 * nz, bins), F32),
-            pltpu.VMEM(((nx - 2) * ny, bins), F32),
+            pltpu.VMEM((total, LANES), BF16),
+            pltpu.VMEM((LANES, bins), BF16),
+            pltpu.VMEM((columns, bins), F32),
             pltpu.VMEM(((nx - 2) * ny, bins), BF16),
             pltpu.VMEM((rim, bins), BF16),
             pltpu.VMEM((rim, bins), F32),
@@ -485,7 +491,7 @@
         name="step",
     )(dense, *winds, fall_rate, listed, block_target, pair_inputs, pair_outputs, loss_kernel, fragments)
 
-    slots = 4
+    slots = 8
     _, settled = pl.pallas_call(
         settle_kernel,
         out_shape=(

time: 31 us -> 28.7 us (0.926)
  Pallas kernels: 30.9 us -> 28.5 us
    pallas_call x1, Pallas kernels: 26.5 us -> 24.3 us  [body(): pl.pallas_call(step_kernel, out_shape=(pltpu.VMEM((halves, cells, LANES),...]
where the time goes in v2:
time: 28.7 us; the launch traced here: 28.5 us
  Pallas kernels  28.5 us (99%)
    pallas_call x1, Pallas kernels, body(): pl.pallas_call(step_kernel, out_shape=(pltpu.VMEM((halves, cells, LANES),...  24.3 us
    pallas_call x1, Pallas kernels, body(): pl.pallas_call(settle_kernel, out_shape=(pltpu.VMEM((halves, cells, LANES...  4.25 us

profile of v2, /device:TPU:0, one launch (start us, length us, event | category | flops | bytes accessed | tf_op | source)
XLA Modules:
  0.0 28.5 jit_solution(6359356068520811056)
XLA Ops:
  0.0 24.3 %step.1 = (f32[2,8192,128]{2,1,0:T(8,128)S(1)}, f32[2,1024,128]{2,1,0:T(8,128)S(1)}, bf16[1024,256]{1,0:T(8,128)(2,1)S(1)}, bf16[128,256]{1,0:T(8,128)(2,1)S(1)}...) custom-call(bf16[32,32,16,128]{3,2,1,0:T(8,128)(2,1)} %bitcast.15, f32[32,8,32]{2,1,0:T(8,128)} %bitcast.16, ...), custom_call_target="tpu_custom_call" | custom-call | tf_op jit(solution)/shard_map/step/pallas_call | solution.py:441
  24.3 4.2 %settle.1 = (f32[2,8192,128]{2,1,0:T(8,128)S(1)}, bf16[32,32,16,128]{3,2,1,0:T(8,128)(2,1)}) custom-call(f32[2,8192,128]{2,1,0:T(8,128)S(1)} %get-tuple-element.12.adv_in, f32[2,1024,128]{2,1,0:T(8,128)S(1)} %get-tuple-element.13.moist, bf16[1024,256]{1,0:T(8,128)(2,1)S(1)} %get-tuple-element.14.arrived, ...), custom_call_target="tpu_custom_call", output_to_operand_aliasing={{0}: (0, {})} | custom-call | tf_op jit(solution)/shard_map/settle/pallas_call | solution.py:495

commit v3 on v2

--- a/solution.py
+++ b/solution.py
@@ -188,7 +188,7 @@
 
     size = min(512, total)
     tile = min(256, pairs)
-    inner = down_sem.shape[0] - 1
+    inner = down_sem.shape[0] - 2
     span = (nx - 2) // inner
     wide = span * ny
 
@@ -241,9 +241,11 @@
         ]
         return total_of(terms)
 
+    edge = {inner: slice(0, 2 * ny), inner + 1: slice(2 * ny, 2 * (ny + nx))}
+
     def down(p):
-        src = edge_flux if p == inner else flux.at[pl.ds(p * wide, wide)]
-        dst = edge_in if p == inner else arrived.at[pl.ds((1 + p * span) * ny, wide)]
+        src = edge_flux.at[edge[p]] if p in edge else flux.at[pl.ds(p * wide, wide)]
+        dst = edge_in.at[edge[p]] if p in edge else arrived.at[pl.ds((1 + p * span) * ny, wide)]
         return pltpu.make_async_remote_copy(
             src_ref=src,
             dst_ref=dst,
@@ -258,8 +260,9 @@
 
         @pl.when(me > 0)
         def _():
-            if p == inner:
-                edge_flux[...] = (edge_flux[...].astype(F32) + edge_in[...].astype(F32) * gain).astype(BF16)
+            if p in edge:
+                at = edge[p]
+                edge_flux[at, :] = (edge_flux[at, :].astype(F32) + edge_in[at, :].astype(F32) * gain).astype(BF16)
             else:
                 at = pl.ds(p * wide, wide)
                 got = arrived[pl.ds((1 + p * span) * ny, wide), :].astype(F32)
@@ -270,11 +273,12 @@
     collide_all()
 
     for p in range(inner):
-        column = lax.broadcasted_iota(I32, (wide, LANES), 0) + (1 + p * span) * ny
-        held = settled[(1 + p * span) * ny : (1 + (p + 1) * span) * ny, :]
-        flux[p * wide : (p + 1) * wide, :] = (collected(column) + held).astype(BF16)
-
-    for p in range(inner):
+        half = wide // 2
+        for part in range(2):
+            start = p * wide + part * half
+            column = lax.broadcasted_iota(I32, (half, LANES), 0) + (ny + start)
+            held = settled[ny + start : ny + start + half, :]
+            flux[start : start + half, :] = (collected(column) + held).astype(BF16)
 
         @pl.when(me == top)
         def _():
@@ -309,42 +313,46 @@
 
     collide_all()
 
-    rim = edge_flux.shape[0]
-    order = lax.broadcasted_iota(I32, (rim, LANES), 0)
-    near = jnp.where(order < ny, order, order - ny + (nx - 1) * ny)
-    far = order - 2 * ny
-    side = jnp.where(far < nx, far * ny, (far - nx) * ny + ny - 1)
-    extra[0:rim, :] = collected(jnp.where(order < 2 * ny, near, side))
-    for r in range(0, rim, GROUP):
-        if r < 2 * ny:
-            x, y = (0, r) if r < ny else (nx - 1, r - ny)
-            base, stride = x * ny + y, 1
+    for p, at in edge.items():
+        order = lax.broadcasted_iota(I32, (at.stop - at.start, LANES), 0)
+        if p == inner:
+            column = jnp.where(order < ny, order, order - ny + (nx - 1) * ny)
         else:
-            x, y = (r - 2 * ny, 0) if r - 2 * ny < nx else (r - 2 * ny - nx, ny - 1)
-            base, stride = x * ny + y, ny
-        for h in range(halves):
-            lanes = slice(h * LANES, (h + 1) * LANES)
-            extra[r : r + GROUP, lanes] = extra[r : r + GROUP, lanes] + drained(base, stride, lanes, h)
-    edge_flux[...] = extra[0:rim, :].astype(BF16)
+            column = jnp.where(order < nx, order * ny, (order - nx) * ny + ny - 1)
+        extra[at, :] = collected(column)
+        for r in range(at.start, at.stop, GROUP):
+            if p == inner:
+                first, apart = (r, 1) if r < ny else (r - ny + (nx - 1) * ny, 1)
+            else:
+                i = r - 2 * ny
+                first, apart = (i * ny, ny) if i < nx else ((i - nx) * ny + ny - 1, ny)
+            for h in range(halves):
+                lanes = slice(h * LANES, (h + 1) * LANES)
+                extra[r : r + GROUP, lanes] = extra[r : r + GROUP, lanes] + drained(first, apart, lanes, h)
+        edge_flux[at, :] = extra[at, :].astype(BF16)
+
+        @pl.when(me == top)
+        def _():
+            down(p).start()
 
     @pl.when(me == top)
     def _():
-        down(inner).start()
         arrived[...] = jnp.zeros(arrived.shape, BF16)
         edge_in[...] = jnp.zeros(edge_in.shape, BF16)
 
     @pl.when(me == top - 1)
     def _():
-        relay(inner)
+        for p in edge:
+            relay(p)
 
     @pl.when(me < top - 1)
     def _():
-        for p in range(inner + 1):
+        for p in range(inner + 2):
             relay(p)
 
     @pl.when(me > 0)
     def _():
-        for p in range(inner + 1):
+        for p in range(inner + 2):
             down(p).wait_send()
 
     for send in sends:
@@ -360,6 +368,7 @@
     halves = bins // LANES
     width, blocks = cells.shape
     slots = level_out.shape[0]
+    each = nx // out_sem.shape[0]
 
     fetch = pltpu.make_async_copy(spots, cells, cell_sem.at[0])
     fetch.start()
@@ -380,7 +389,7 @@
             adv[h, cell, :] = moist[h, r : r + 1, :]
 
     def push(i):
-        at = pl.ds(i * slots, slots)
+        at = pl.ds(i * each, each)
         return pltpu.make_async_copy(staged.at[at], out.at[at], out_sem.at[i])
 
     def some_rows(i, carry):
@@ -399,11 +408,12 @@
             for y in range(ny):
                 pieces = [level_out[slot, h, y * nz : (y + 1) * nz, :] for h in range(halves)]
                 staged[x, y] = jnp.concatenate(pieces, axis=0).astype(BF16)
-        push(i).start()
+            if (slot + 1) % each == 0:
+                push((x + 1) // each - 1).start()
         return carry
 
     lax.fori_loop(0, nx // slots, some_rows, 0)
-    for i in range(nx // slots):
+    for i in range(nx // each):
         push(i).wait()
 
 
@@ -433,7 +443,7 @@
     hbm = pl.BlockSpec(memory_space=pltpu.HBM)
     vmem = pl.BlockSpec(memory_space=pltpu.VMEM)
     dense = spectrum.reshape(nx, ny, nz, halves, LANES).transpose(0, 1, 3, 2, 4).reshape(nx, ny, packed, LANES)
-    span = max(s for s in range(1, 11) if (nx - 2) % s == 0)
+    span = max(s for s in range(1, 7) if (nx - 2) % s == 0)
     inner = (nx - 2) // span
     rim = 2 * (nx + ny)
     parts = 4
@@ -482,8 +492,8 @@
             dma((1,)),
             dma((4,)),
             dma((4,)),
-            dma((inner + 1,)),
-            dma((inner + 1,)),
+            dma((inner + 2,)),
+            dma((inner + 2,)),
         ],
         compiler_params=pltpu.CompilerParams(
             collective_id=0, has_side_effects=True, vmem_limit_bytes=(60 << 20) - cells * bins * 4
@@ -508,7 +518,7 @@
             pltpu.VMEM((slots, halves, ny * nz, LANES), F32),
             pltpu.VMEM((nx, ny, packed, LANES), BF16),
             dma((1,)),
-            dma((nx // slots,)),
+            dma((nx // 2,)),
         ],
         input_output_aliases={0: 0},
         compiler_params=pltpu.CompilerParams(vmem_limit_bytes=32 << 20),

time: 28.7 us -> 28.7 us (level)
  no operation moved by 1% of the time
where the time goes in v3:
time: 28.7 us; the launch traced here: 28.6 us
  Pallas kernels  28.6 us (100%)
    pallas_call x1, Pallas kernels, body(): pl.pallas_call(step_kernel, out_shape=(pltpu.VMEM((halves, cells, LANES),...  24.4 us
    pallas_call x1, Pallas kernels, body(): pl.pallas_call(settle_kernel, out_shape=(pltpu.VMEM((halves, cells, LANES...  4.11 us

profile of v3, /device:TPU:0, one launch (start us, length us, event | category | flops | bytes accessed | tf_op | source)
XLA Modules:
  0.0 28.6 jit_solution(1155359563738221571)
XLA Ops:
  0.0 24.4 %step.1 = (f32[2,8192,128]{2,1,0:T(8,128)S(1)}, f32[2,1024,128]{2,1,0:T(8,128)S(1)}, bf16[1024,256]{1,0:T(8,128)(2,1)S(1)}, bf16[128,256]{1,0:T(8,128)(2,1)S(1)}...) custom-call(bf16[32,32,16,128]{3,2,1,0:T(8,128)(2,1)} %bitcast.15, f32[32,8,32]{2,1,0:T(8,128)} %bitcast.16, ...), custom_call_target="tpu_custom_call" | custom-call | tf_op jit(solution)/shard_map/step/pallas_call | solution.py:451
  24.5 4.1 %settle.1 = (f32[2,8192,128]{2,1,0:T(8,128)S(1)}, bf16[32,32,16,128]{3,2,1,0:T(8,128)(2,1)}) custom-call(f32[2,8192,128]{2,1,0:T(8,128)S(1)} %get-tuple-element.12.adv_in, f32[2,1024,128]{2,1,0:T(8,128)S(1)} %get-tuple-element.13.moist, bf16[1024,256]{1,0:T(8,128)(2,1)S(1)} %get-tuple-element.14.arrived, ...), custom_call_target="tpu_custom_call", output_to_operand_aliasing={{0}: (0, {})} | custom-call | tf_op jit(solution)/shard_map/settle/pallas_call | solution.py:505

commit v4 on v3

--- a/solution.py
+++ b/solution.py
@@ -21,9 +21,9 @@
 
 def step_kernel(
     spec, winds_e, winds_n, fall_h, cells_h, target_h, pair_in_h, pair_out_h, loss_h, frag_h,
-    adv, moist, arrived, edge_in, spots, fall,
+    adv, moist, edge_moist, arrived, edge_in, spots, fall,
     local, we, wn, west, east, south, north, cells, listed_v, target, pair_in, pair_out, loss, frag,
-    rows, q, pz, ids, live, shares, picks, table, settled, flux, edge_flux, extra,
+    rows, q, pz, ids, places, live, shares, picks, table, settled, flux, edge_flux,
     load_sem, in_sem, spot_sem, send_sem, recv_sem, down_sem, got_sem,
 ):
     nx, ny, packed, _ = spec.shape
@@ -157,11 +157,12 @@
     spot.start()
     cloudy = target[gx, gy] < plane
     columns = jnp.where(cloudy, listed // nz, -1)
+    cloudy_spots = jnp.where(cloudy, spots[...], -1)
     per_tile = LANES // blocks
     for t in range(total // LANES):
-        ids[t : t + 1, :] = jnp.concatenate(
-            [columns[t * per_tile + i : t * per_tile + i + 1, :] for i in range(per_tile)], axis=1
-        )
+        for kept, found in ((ids, columns), (places, cloudy_spots)):
+            lines = [found[t * per_tile + i : t * per_tile + i + 1, :] for i in range(per_tile)]
+            kept[t : t + 1, :] = jnp.concatenate(lines, axis=1)
     flags = jnp.broadcast_to(jnp.where(cloudy, 1.0, 0.0), (8, blocks)).T
     live[...] = jnp.broadcast_to(flags[:, 0:1], (blocks, LANES))
     heights = (listed % nz).astype(F32).T
@@ -198,10 +199,7 @@
             for h in range(halves):
                 rows[h, r : r + 1, :] = adv[h, cell, :]
 
-    def collide(i):
-        at = slice(i * size, (i + 1) * size)
-        full = jnp.concatenate([rows[h, at, :] for h in range(halves)], axis=1)
-        row = full.astype(BF16)
+    def tendency_of(row):
         decline = jnp.dot(row, loss[...], preferred_element_type=F32)
         losses = row.astype(F32) * decline
         gained = jnp.dot(losses.astype(BF16), frag[...], preferred_element_type=F32)
@@ -210,13 +208,57 @@
             second = jnp.dot(row, pair_in[:, pairs + n : pairs + n + tile], preferred_element_type=F32)
             product = (first * second).astype(BF16)
             gained = gained + jnp.dot(product, pair_out[n : n + tile, :], preferred_element_type=F32)
-        tendency = (gained - losses).astype(BF16).astype(F32)
+        return (gained - losses).astype(BF16).astype(F32)
+
+    def collide(i):
+        at = slice(i * size, (i + 1) * size)
+        full = jnp.concatenate([rows[h, at, :] for h in range(halves)], axis=1)
         alive = jnp.concatenate([jnp.concatenate([live[...]] * halves, axis=1)] * (size // blocks), axis=0)
-        tendency = jnp.where(alive > 0.0, tendency, 0.0)
+        tendency = jnp.where(alive > 0.0, tendency_of(full.astype(BF16)), 0.0)
         q[at, :] = (tendency * pz[at, :]).astype(BF16)
         after = full + tendency
         for h in range(halves):
             moist[h, at, :] = after[:, h * LANES : (h + 1) * LANES]
+
+    def listed_tile(first, apart):
+        cell = lax.broadcasted_iota(I32, (GROUP, LANES), 0) * apart + first
+        hit = jnp.broadcast_to(places[0:1, :], cell.shape) == cell
+        for t in range(1, total // LANES):
+            hit = hit | (jnp.broadcast_to(places[t : t + 1, :], cell.shape) == cell)
+        found = jnp.max(jnp.where(hit, 1.0, 0.0), axis=1, keepdims=True)
+        return jnp.broadcast_to(found, cell.shape)
+
+    def rim_tiles(p):
+        if p == inner:
+            starts = [x * ny * nz + k * GROUP for x in (0, nx - 1) for k in range(ny * nz // GROUP)]
+            return [(start, 1) for start in starts]
+        return [(spot_of(x * ny + y, 0, nz), GROUP) for y in (0, ny - 1) for x in range(nx)]
+
+    def collide_rim(p):
+        tiles = rim_tiles(p)
+        sides = []
+        for h in range(halves):
+            if p == inner:
+                wanted = [adv[h, x * ny * nz : (x + 1) * ny * nz, :] for x in (0, nx - 1)]
+            else:
+                wanted = [adv[h, pl.ds(first, nz, stride=apart), :] for first, apart in tiles]
+            sides.append(jnp.concatenate(wanted, axis=0))
+        full = jnp.concatenate(sides, axis=1)
+        alive = jnp.concatenate([listed_tile(first, apart) for first, apart in tiles], axis=0)
+        alive = jnp.concatenate([alive] * halves, axis=1)
+        after = full + jnp.where(alive > 0.0, tendency_of(full.astype(BF16)), 0.0)
+        offset = 0 if p == inner else 2 * ny * nz
+        for h in range(halves):
+            edge_moist[h, offset : offset + full.shape[0], :] = after[:, h * LANES : (h + 1) * LANES]
+        left = []
+        if p == inner:
+            for g in range(2 * ny // GROUP):
+                level = [after[(g * nz + z) * GROUP : (g * nz + z + 1) * GROUP, :] * shares[z : z + 1, :] for z in range(nz)]
+                left.append(total_of(level))
+        else:
+            for i in range(2 * nx):
+                left.append(jnp.sum(after[i * nz : (i + 1) * nz, :] * shares[0:nz, :], axis=0, keepdims=True))
+        edge_flux[edge[p], :] = jnp.concatenate(left, axis=0).astype(BF16)
 
     def collide_all():
         chunks = total // size
@@ -232,14 +274,6 @@
             for t in range(total // LANES)
         ]
         return jnp.dot(jnp.concatenate(hot, axis=1), q[...], preferred_element_type=F32)
-
-    def drained(column, apart, lanes, h):
-        first = spot_of(column, 0, nz)
-        stride = 1 if apart == 1 else apart * nz
-        terms = [
-            adv[h, pl.ds(first + z * GROUP, GROUP, stride=stride), :] * shares[z : z + 1, lanes] for z in range(nz)
-        ]
-        return total_of(terms)
 
     edge = {inner: slice(0, 2 * ny), inner + 1: slice(2 * ny, 2 * (ny + nx))}
 
@@ -311,25 +345,8 @@
         for y in range(ny):
             add_halo(x * ny + y, spread(winds, y), halo[y])
 
-    collide_all()
-
-    for p, at in edge.items():
-        order = lax.broadcasted_iota(I32, (at.stop - at.start, LANES), 0)
-        if p == inner:
-            column = jnp.where(order < ny, order, order - ny + (nx - 1) * ny)
-        else:
-            column = jnp.where(order < nx, order * ny, (order - nx) * ny + ny - 1)
-        extra[at, :] = collected(column)
-        for r in range(at.start, at.stop, GROUP):
-            if p == inner:
-                first, apart = (r, 1) if r < ny else (r - ny + (nx - 1) * ny, 1)
-            else:
-                i = r - 2 * ny
-                first, apart = (i * ny, ny) if i < nx else ((i - nx) * ny + ny - 1, ny)
-            for h in range(halves):
-                lanes = slice(h * LANES, (h + 1) * LANES)
-                extra[r : r + GROUP, lanes] = extra[r : r + GROUP, lanes] + drained(first, apart, lanes, h)
-        edge_flux[at, :] = extra[at, :].astype(BF16)
+    for p in edge:
+        collide_rim(p)
 
         @pl.when(me == top)
         def _():
@@ -360,7 +377,7 @@
 
 
 def settle_kernel(
-    adv_in, moist, arrived, edge_in, spots, fall, adv, out, cells, flow, inverse, ratio, level_out, staged,
+    adv_in, moist, edge_moist, arrived, edge_in, spots, fall, adv, out, cells, flow, inverse, ratio, level_out, staged,
     cell_sem, out_sem
 ):
     nx, ny, packed, _ = out.shape
@@ -387,6 +404,15 @@
         cell = pl.ds(cells[r // blocks, r % blocks], 1)
         for h in range(halves):
             adv[h, cell, :] = moist[h, r : r + 1, :]
+
+    row = ny * nz
+    for h in range(halves):
+        for i, x in enumerate((0, nx - 1)):
+            adv[h, x * row : (x + 1) * row, :] = edge_moist[h, i * row : (i + 1) * row, :]
+        for i, y in enumerate((0, ny - 1)):
+            for x in range(nx):
+                came = (2 * ny + i * nx + x) * nz
+                adv[h, pl.ds(spot_of(x * ny + y, 0, nz), nz, stride=GROUP), :] = edge_moist[h, came : came + nz, :]
 
     def push(i):
         at = pl.ds(i * each, each)
@@ -448,18 +474,19 @@
     rim = 2 * (nx + ny)
     parts = 4
 
-    adv, moist, arrived, edge_in, spots, fall_v = pl.pallas_call(
+    adv, moist, edge_moist, arrived, edge_in, spots, fall_v = pl.pallas_call(
         step_kernel,
         out_shape=(
             pltpu.VMEM((halves, cells, LANES), F32),
             pltpu.VMEM((halves, total, LANES), F32),
+            pltpu.VMEM((halves, rim * nz, LANES), F32),
             pltpu.VMEM((columns, bins), BF16),
             pltpu.VMEM((rim, bins), BF16),
             pltpu.VMEM((width, blocks), I32),
             pltpu.VMEM(fall_rate.shape, F32),
         ),
         in_specs=[hbm] * 10,
-        out_specs=(vmem,) * 6,
+        out_specs=(vmem,) * 7,
         scratch_shapes=[
             pltpu.VMEM((nx + 2, ny, packed, LANES), BF16),
             pltpu.VMEM(winds[0].shape, F32),
@@ -479,6 +506,7 @@
             pltpu.VMEM((total, bins), BF16),
             pltpu.VMEM((total, bins), F32),
             pltpu.VMEM((max(total // LANES, 8), LANES), I32),
+            pltpu.VMEM((max(total // LANES, 8), LANES), I32),
             pltpu.VMEM((blocks, LANES), F32),
             pltpu.VMEM((2 * nz, bins), F32),
             pltpu.VMEM((total, LANES), BF16),
@@ -486,7 +514,6 @@
             pltpu.VMEM((columns, bins), F32),
             pltpu.VMEM(((nx - 2) * ny, bins), BF16),
             pltpu.VMEM((rim, bins), BF16),
-            pltpu.VMEM((rim, bins), F32),
             dma((parts,)),
             dma((10,)),
             dma((1,)),
@@ -508,7 +535,7 @@
             pltpu.VMEM((halves, cells, LANES), F32),
             jax.ShapeDtypeStruct((nx, ny, packed, LANES), BF16),
         ),
-        in_specs=[vmem] * 6,
+        in_specs=[vmem] * 7,
         out_specs=(vmem, hbm),
         scratch_shapes=[
             pltpu.SMEM((width, blocks), I32),
@@ -523,7 +550,7 @@
         input_output_aliases={0: 0},
         compiler_params=pltpu.CompilerParams(vmem_limit_bytes=32 << 20),
         name="settle",
-    )(adv, moist, arrived, edge_in, spots, fall_v)
+    )(adv, moist, edge_moist, arrived, edge_in, spots, fall_v)
     return settled.reshape(nx, ny, halves, nz, LANES).transpose(0, 1, 3, 2, 4).reshape(nx, ny, nz, bins)
 
 

time: 28.7 us -> 28.2 us (0.983)
  Pallas kernels: 28.6 us -> 28 us
    pallas_call x1, Pallas kernels: 24.4 us -> 23.7 us  [body(): pl.pallas_call(step_kernel, out_shape=(pltpu.VMEM((halves, cells, LANES),...]
where the time goes in v4:
time: 28.2 us; the launch traced here: 28 us
  Pallas kernels  28 us (99%)
    pallas_call x1, Pallas kernels, body(): pl.pallas_call(step_kernel, out_shape=(pltpu.VMEM((halves, cells, LANES),...  23.7 us
    pallas_call x1, Pallas kernels, body(): pl.pallas_call(settle_kernel, out_shape=(pltpu.VMEM((halves, cells, LANES...  4.29 us

profile of v4, /device:TPU:0, one launch (start us, length us, event | category | flops | bytes accessed | tf_op | source)
XLA Modules:
  0.0 28.0 jit_solution(10174659664847944811)
XLA Ops:
  0.0 23.7 %step.1 = (f32[2,8192,128]{2,1,0:T(8,128)S(1)}, f32[2,1024,128]{2,1,0:T(8,128)S(1)}, f32[2,1024,128]{2,1,0:T(8,128)S(1)}, bf16[1024,256]{1,0:T(8,128)(2,1)S(1)},...) custom-call(bf16[32,32,16,128]{3,2,1,0:T(8,128)(2,1)} %bitcast.15, ...), custom_call_target="tpu_custom_call" | custom-call | tf_op jit(solution)/shard_map/step/pallas_call | solution.py:477
  23.7 4.3 %settle.1 = (f32[2,8192,128]{2,1,0:T(8,128)S(1)}, bf16[32,32,16,128]{3,2,1,0:T(8,128)(2,1)}) custom-call(f32[2,8192,128]{2,1,0:T(8,128)S(1)} %get-tuple-element.13.adv_in, f32[2,1024,128]{2,1,0:T(8,128)S(1)} %get-tuple-element.14.moist, f32[2,1024,128]{2,1,0:T(8,128)S(1)} %get-tuple-element.15.edge_moist, ...), custom_call_target="tpu_custom_call", output_to_operand_aliasing={{0}: (0, {})} | custom-call | tf_op jit(solution)/shard_map/settle/pallas_call | solution.py:532

commit v5 on v4

--- a/solution.py
+++ b/solution.py
@@ -348,12 +348,10 @@
     for p in edge:
         collide_rim(p)
 
-        @pl.when(me == top)
-        def _():
-            down(p).start()
-
     @pl.when(me == top)
     def _():
+        for p in edge:
+            down(p).start()
         arrived[...] = jnp.zeros(arrived.shape, BF16)
         edge_in[...] = jnp.zeros(edge_in.shape, BF16)
 
@@ -469,7 +467,7 @@
     hbm = pl.BlockSpec(memory_space=pltpu.HBM)
     vmem = pl.BlockSpec(memory_space=pltpu.VMEM)
     dense = spectrum.reshape(nx, ny, nz, halves, LANES).transpose(0, 1, 3, 2, 4).reshape(nx, ny, packed, LANES)
-    span = max(s for s in range(1, 7) if (nx - 2) % s == 0)
+    span = max(s for s in range(1, 11) if (nx - 2) % s == 0)
     inner = (nx - 2) // span
     rim = 2 * (nx + ny)
     parts = 4

time: 28.2 us -> 28.3 us (level)
  no operation moved by 1% of the time
where the time goes in v5:
time: 28.3 us; the launch traced here: 28.1 us
  Pallas kernels  28.1 us (99%)
    pallas_call x1, Pallas kernels, body(): pl.pallas_call(step_kernel, out_shape=(pltpu.VMEM((halves, cells, LANES),...  23.8 us
    pallas_call x1, Pallas kernels, body(): pl.pallas_call(settle_kernel, out_shape=(pltpu.VMEM((halves, cells, LANES...  4.29 us

profile of v5, /device:TPU:0, one launch (start us, length us, event | category | flops | bytes accessed | tf_op | source)
XLA Modules:
  0.0 28.1 jit_solution(9044993205082876980)
XLA Ops:
  0.0 23.8 %step.1 = (f32[2,8192,128]{2,1,0:T(8,128)S(1)}, f32[2,1024,128]{2,1,0:T(8,128)S(1)}, f32[2,1024,128]{2,1,0:T(8,128)S(1)}, bf16[1024,256]{1,0:T(8,128)(2,1)S(1)},...) custom-call(bf16[32,32,16,128]{3,2,1,0:T(8,128)(2,1)} %bitcast.15, ...), custom_call_target="tpu_custom_call" | custom-call | tf_op jit(solution)/shard_map/step/pallas_call | solution.py:475
  23.8 4.3 %settle.1 = (f32[2,8192,128]{2,1,0:T(8,128)S(1)}, bf16[32,32,16,128]{3,2,1,0:T(8,128)(2,1)}) custom-call(f32[2,8192,128]{2,1,0:T(8,128)S(1)} %get-tuple-element.13.adv_in, f32[2,1024,128]{2,1,0:T(8,128)S(1)} %get-tuple-element.14.moist, f32[2,1024,128]{2,1,0:T(8,128)S(1)} %get-tuple-element.15.edge_moist, ...), custom_call_target="tpu_custom_call", output_to_operand_aliasing={{0}: (0, {})} | custom-call | tf_op jit(solution)/shard_map/settle/pallas_call | solution.py:530

commit v6 on v5

--- a/solution.py
+++ b/solution.py
@@ -467,7 +467,7 @@
     hbm = pl.BlockSpec(memory_space=pltpu.HBM)
     vmem = pl.BlockSpec(memory_space=pltpu.VMEM)
     dense = spectrum.reshape(nx, ny, nz, halves, LANES).transpose(0, 1, 3, 2, 4).reshape(nx, ny, packed, LANES)
-    span = max(s for s in range(1, 11) if (nx - 2) % s == 0)
+    span = max(s for s in range(1, 6) if (nx - 2) % s == 0)
     inner = (nx - 2) // span
     rim = 2 * (nx + ny)
     parts = 4

time: 28.3 us -> 28.1 us (level)
  no operation moved by 1% of the time
where the time goes in v6:
time: 28.1 us; the launch traced here: 28 us
  Pallas kernels  28 us (100%)
    pallas_call x1, Pallas kernels, body(): pl.pallas_call(step_kernel, out_shape=(pltpu.VMEM((halves, cells, LANES),...  23.7 us
    pallas_call x1, Pallas kernels, body(): pl.pallas_call(settle_kernel, out_shape=(pltpu.VMEM((halves, cells, LANES...  4.29 us

profile of v6, /device:TPU:0, one launch (start us, length us, event | category | flops | bytes accessed | tf_op | source)
XLA Modules:
  0.0 28.0 jit_solution(17883296229656560240)
XLA Ops:
  0.0 23.7 %step.1 = (f32[2,8192,128]{2,1,0:T(8,128)S(1)}, f32[2,1024,128]{2,1,0:T(8,128)S(1)}, f32[2,1024,128]{2,1,0:T(8,128)S(1)}, bf16[1024,256]{1,0:T(8,128)(2,1)S(1)},...) custom-call(bf16[32,32,16,128]{3,2,1,0:T(8,128)(2,1)} %bitcast.15, ...), custom_call_target="tpu_custom_call" | custom-call | tf_op jit(solution)/shard_map/step/pallas_call | solution.py:475
  23.7 4.3 %settle.1 = (f32[2,8192,128]{2,1,0:T(8,128)S(1)}, bf16[32,32,16,128]{3,2,1,0:T(8,128)(2,1)}) custom-call(f32[2,8192,128]{2,1,0:T(8,128)S(1)} %get-tuple-element.13.adv_in, f32[2,1024,128]{2,1,0:T(8,128)S(1)} %get-tuple-element.14.moist, f32[2,1024,128]{2,1,0:T(8,128)S(1)} %get-tuple-element.15.edge_moist, ...), custom_call_target="tpu_custom_call", output_to_operand_aliasing={{0}: (0, {})} | custom-call | tf_op jit(solution)/shard_map/settle/pallas_call | solution.py:530

commit v7 on v6

--- a/solution.py
+++ b/solution.py
@@ -543,7 +543,7 @@
             pltpu.VMEM((slots, halves, ny * nz, LANES), F32),
             pltpu.VMEM((nx, ny, packed, LANES), BF16),
             dma((1,)),
-            dma((nx // 2,)),
+            dma((nx // 4,)),
         ],
         input_output_aliases={0: 0},
         compiler_params=pltpu.CompilerParams(vmem_limit_bytes=32 << 20),

time: 28.1 us -> 28.2 us (level)
  no operation moved by 1% of the time
where the time goes in v7:
time: 28.2 us; the launch traced here: 28 us
  Pallas kernels  28 us (99%)
    pallas_call x1, Pallas kernels, body(): pl.pallas_call(step_kernel, out_shape=(pltpu.VMEM((halves, cells, LANES),...  23.7 us
    pallas_call x1, Pallas kernels, body(): pl.pallas_call(settle_kernel, out_shape=(pltpu.VMEM((halves, cells, LANES...  4.29 us

profile of v7, /device:TPU:0, one launch (start us, length us, event | category | flops | bytes accessed | tf_op | source)
XLA Modules:
  0.0 28.0 jit_solution(6354207673879768871)
XLA Ops:
  0.0 23.7 %step.1 = (f32[2,8192,128]{2,1,0:T(8,128)S(1)}, f32[2,1024,128]{2,1,0:T(8,128)S(1)}, f32[2,1024,128]{2,1,0:T(8,128)S(1)}, bf16[1024,256]{1,0:T(8,128)(2,1)S(1)},...) custom-call(bf16[32,32,16,128]{3,2,1,0:T(8,128)(2,1)} %bitcast.15, ...), custom_call_target="tpu_custom_call" | custom-call | tf_op jit(solution)/shard_map/step/pallas_call | solution.py:475
  23.7 4.3 %settle.1 = (f32[2,8192,128]{2,1,0:T(8,128)S(1)}, bf16[32,32,16,128]{3,2,1,0:T(8,128)(2,1)}) custom-call(f32[2,8192,128]{2,1,0:T(8,128)S(1)} %get-tuple-element.13.adv_in, f32[2,1024,128]{2,1,0:T(8,128)S(1)} %get-tuple-element.14.moist, f32[2,1024,128]{2,1,0:T(8,128)S(1)} %get-tuple-element.15.edge_moist, ...), custom_call_target="tpu_custom_call", output_to_operand_aliasing={{0}: (0, {})} | custom-call | tf_op jit(solution)/shard_map/settle/pallas_call | solution.py:530
